TPU v7x, 256 devices: a whole 4x4x8 slice. The times are simulated.
256 devices in a mesh: row: 32 (over x, z), col: 8 (over y, core).
Axes of the slice: x: 4, y: 4, z: 8, core: 2. Of those that a mesh axis runs over, the one named last changes fastest.
Arguments:
- panel_block: float32 [16384, 128], P('row'), may hold values from -8 to 8, as said below
- trailing: float32 [16384, 16384], P('row', 'col'), may hold values from -80 to 80
Outputs:
- reduced: float32 [16384, 16384], P('row', 'col')
- band_block: float32 [128, 128], replicated
- first_factor: float32 [128, 128], replicated
Inputs may be any that keep to these rules, and one draw needn't show every extreme that they name: `panel_block`: entries of order the inverse square root of 16384; rows may differ in scale; the columns may be nearly dependent, with a condition number of the panel up to a few thousand; the first 128 rows of the orthonormal basis have spectral norm at most 0.8, so that I + top^T needs no pivoting.
All inputs are finite; a program needn't handle non-finite values.
Results may differ from a plain program's by a relative error of at most 0.0017.
Values sent between devices are 32-bit elements; how exact they have to be, the bound alone decides.
A program may use at most 128 MiB of HBM per device.

v0:
```python
import jax
import jax.numpy as jnp
from jax import lax
from jax.sharding import PartitionSpec as P

HIGH = lax.Precision.HIGHEST


def broadcast(shard, axis, root):
    mine = lax.axis_index(axis) == root
    return lax.psum(jnp.where(mine, shard, jnp.zeros_like(shard)), axis)


def gram_of(values):
    return lax.dot_general(
        values, values, (((0,), (0,)), ((), ())), precision=HIGH, preferred_element_type=jnp.float32
    )


def times_of(left, right):
    return jnp.dot(left, right, precision=HIGH, preferred_element_type=jnp.float32)


def outer_of(left, right):
    return lax.dot_general(
        left, right, (((1,), (1,)), ((), ())), precision=HIGH, preferred_element_type=jnp.float32
    )


def gram_both(left, right):
    return lax.dot_general(
        left, right, (((0,), (0,)), ((), ())), precision=HIGH, preferred_element_type=jnp.float32
    )


def eliminate_small(square):
    size_n = square.shape[0]
    augmented = jnp.concatenate([square, jnp.eye(size_n, dtype=square.dtype)], axis=1)
    positions = jnp.arange(size_n)

    def eliminate(pivot, current):
        pivot_row = lax.dynamic_index_in_dim(current, pivot, 0, keepdims=False)
        pivot_row = pivot_row / pivot_row[pivot]
        column = lax.dynamic_index_in_dim(current, pivot, 1, keepdims=False)
        column = column - (positions == pivot).astype(current.dtype)
        return current - column[:, None] * pivot_row[None, :]

    augmented = lax.fori_loop(0, size_n, eliminate, augmented)
    return augmented[:, size_n:]


def invert_square(square):
    size_n = square.shape[0]
    if size_n <= 16:
        return eliminate_small(square)
    half = size_n // 2
    upper_left = square[:half, :half]
    upper_right = square[:half, half:]
    lower_left = square[half:, :half]
    lower_right = square[half:, half:]
    left_inverse = invert_square(upper_left)
    left_times_right = times_of(left_inverse, upper_right)
    lower_times_left = times_of(lower_left, left_inverse)
    schur = lower_right - times_of(lower_left, left_times_right)
    schur_inverse = invert_square(schur)
    top_right = -times_of(left_times_right, schur_inverse)
    bottom_left = -times_of(schur_inverse, lower_times_left)
    top_left = left_inverse - times_of(top_right, lower_times_left)
    upper = jnp.concatenate([top_left, top_right], axis=1)
    lower = jnp.concatenate([bottom_left, schur_inverse], axis=1)
    return jnp.concatenate([upper, lower], axis=0)


def right_solve(factor, values):
    return lax.linalg.triangular_solve(
        factor, values, left_side=False, lower=True, transpose_a=True
    )


def body(panel_block, trailing):
    shard_rows = panel_block.shape[0]
    panel_width = panel_block.shape[1]
    col_count = trailing.shape[1]
    row_index = lax.axis_index("row")
    col_index = lax.axis_index("col")
    first_gram = lax.psum(gram_of(panel_block), "row")
    first_factor = jnp.linalg.cholesky(first_gram)
    first_basis = right_solve(first_factor, panel_block)
    second_gram = lax.psum(gram_of(first_basis), "row")
    second_factor = jnp.linalg.cholesky(second_gram)
    basis = right_solve(second_factor, first_basis)
    top_basis = broadcast(basis[:panel_width], "row", 0)
    band_block = -times_of(second_factor.T, first_factor.T)
    kernel = invert_square(jnp.eye(panel_width, dtype=jnp.float32) + top_basis.T)
    global_rows = row_index * shard_rows + jnp.arange(shard_rows)
    ident = (global_rows[:, None] == jnp.arange(panel_width)[None, :]).astype(jnp.float32)
    vectors = basis + ident
    all_vectors = lax.all_gather(vectors, "row", axis=0, tiled=True)
    col_vectors = lax.dynamic_slice_in_dim(all_vectors, col_index * col_count, col_count, 0)
    partial_product = times_of(trailing, col_vectors)
    row_product = lax.psum(partial_product, "col")
    applied = times_of(row_product, kernel)
    inner_sum = lax.psum(gram_both(vectors, applied), "row")
    inner = times_of(kernel.T, inner_sum)
    row_update = applied - 0.5 * times_of(vectors, inner)
    all_update = lax.all_gather(row_update, "row", axis=0, tiled=True)
    col_update = lax.dynamic_slice_in_dim(all_update, col_index * col_count, col_count, 0)
    reduced = trailing - outer_of(vectors, col_update) - outer_of(row_update, col_vectors)
    return (reduced, band_block, first_factor)


def solution(mesh):
    in_specs = (P("row", None), P("row", "col"))
    out_specs = (P("row", "col"), P(), P())
    return jax.shard_map(body, mesh=mesh, in_specs=in_specs, out_specs=out_specs, check_vma=False)
```

profile of v0, /device:TPU:1, one launch (start us, length us, event | category | flops | bytes accessed | tf_op | source)
XLA Modules:
  0.0 1025.3 jit_solution(8369350252822602380)
XLA Ops:
  7.2 0.9 copy-done
  8.1 1.2 fusion.134
  9.4 143.5 %all-reduce.6.cloned.1.call-done = f32[128,128]{0,1:T(8,128)} async-done(((f32[128,128]{0,1:T(8,128)}), f32[128,128]{0,1:T(8,128)}) %all-reduce.6.cloned.1.call-update) | async-done | bytes 65552 | tf_op jit(solution)/shard_map/psum | solution.py:86
  152.9 0.9 copy.26
  153.9 0.9 fusion.57
  154.7 11.7 %cholesky.44 = f32[128,128]{1,0:T(8,128)S(1)} custom-call(f32[128,128]{1,0:T(8,128)S(1)} %fusion.57), custom_call_target="Cholesky" | custom-call | tf_op jit(solution)/shard_map/jit(cholesky)/cholesky | solution.py:87
  167.8 9.8 custom-call.6
  178.0 1.0 fusion.135
  179.3 139.5 %all-reduce.8.cloned.1.call-done = f32[128,128]{0,1:T(8,128)} async-done(((f32[128,128]{0,1:T(8,128)}), f32[128,128]{0,1:T(8,128)}) %all-reduce.8.cloned.1.call-update) | async-done | bytes 65552 | tf_op jit(solution)/shard_map/psum | solution.py:89
  318.8 0.9 copy.28
  319.7 0.9 fusion.55
  320.6 11.7 %cholesky.55 = f32[128,128]{1,0:T(8,128)S(1)} custom-call(f32[128,128]{1,0:T(8,128)S(1)} %fusion.55), custom_call_target="Cholesky" | custom-call | tf_op jit(solution)/shard_map/jit(cholesky)/cholesky | solution.py:90
  333.5 9.8 custom-call.7
  343.3 1.1 convert_add_fusion
  346.0 138.9 %all-reduce.12.cloned.1.call-done = f32[128,128]{1,0:T(8,128)} async-done(((f32[128,128]{1,0:T(8,128)}), f32[128,128]{1,0:T(8,128)}) %all-reduce.12.cloned.1.call-update) | async-done | bytes 65552 | tf_op jit(solution)/shard_map/psum | solution.py:11
  484.9 0.9 fusion.65
  485.9 24.0 %while.136 = (s32[]{:T(128)}, f32[16,32]{0,1:T(8,128)S(1)}, s32[]{:T(128)}, s32[]{:T(128)}, s32[]{:T(128)}, /*index=5*/s32[]{:T(128)}) while((s32[]{:T(128)}, f32[16,32]{0,1:T(8,128)S(1)}, s32[]{:T(128)}, s32[]{:T(128)}, s32[]{:T(128)}, /*index=5*/s32[]{:T(128)}) %tuple.325), condition=%wide.region_7.10_spmd.clone, body=%wide.region_6.9_spmd.clone.sunk | while | flops 1108 | bytes 5825 | solution.py:48
  501.5 0.8 fusion.206
  503.0 0.8 fusion.206
  506.0 0.8 fusion.206
  509.1 0.8 fusion.206
  510.8 24.0 %while.137 = (s32[]{:T(128)}, f32[16,32]{0,1:T(8,128)S(1)}, s32[]{:T(128)}, s32[]{:T(128)}, s32[]{:T(128)}, /*index=5*/s32[]{:T(128)}) while((s32[]{:T(128)}, f32[16,32]{0,1:T(8,128)S(1)}, s32[]{:T(128)}, s32[]{:T(128)}, s32[]{:T(128)}, /*index=5*/s32[]{:T(128)}) %tuple.328), condition=%wide.region_9.12_spmd.clone, body=%wide.region_8.11_spmd.clone.sunk | while | flops 1108 | bytes 5825 | solution.py:48
  515.8 0.8 fusion.208
  520.3 0.8 fusion.208
  521.8 0.8 fusion.208
  536.2 24.0 %while.138 = (s32[]{:T(128)}, f32[16,32]{0,1:T(8,128)S(1)}, s32[]{:T(128)}, s32[]{:T(128)}, s32[]{:T(128)}, /*index=5*/s32[]{:T(128)}) while((s32[]{:T(128)}, f32[16,32]{0,1:T(8,128)S(1)}, s32[]{:T(128)}, s32[]{:T(128)}, s32[]{:T(128)}, /*index=5*/s32[]{:T(128)}) %tuple.331), condition=%wide.region_11.14_spmd.clone, body=%wide.region_10.13_spmd.clone.sunk | while | flops 1108 | bytes 5825 | solution.py:48
  539.8 0.8 fusion.210
  541.3 0.8 fusion.210
  553.4 0.8 fusion.210
  556.4 0.8 fusion.210
  561.1 24.0 %while.139 = (s32[]{:T(128)}, f32[16,32]{0,1:T(8,128)S(1)}, s32[]{:T(128)}, s32[]{:T(128)}, s32[]{:T(128)}, /*index=5*/s32[]{:T(128)}) while((s32[]{:T(128)}, f32[16,32]{0,1:T(8,128)S(1)}, s32[]{:T(128)}, s32[]{:T(128)}, s32[]{:T(128)}, /*index=5*/s32[]{:T(128)}) %tuple.334), condition=%wide.region_13.16_spmd.clone, body=%wide.region_12.15_spmd.clone.sunk | while | flops 1108 | bytes 5825 | solution.py:48
  561.7 0.8 fusion.212
  567.7 0.8 fusion.212
  587.1 24.0 %while.140 = (s32[]{:T(128)}, f32[16,32]{0,1:T(8,128)S(1)}, s32[]{:T(128)}, s32[]{:T(128)}, s32[]{:T(128)}, /*index=5*/s32[]{:T(128)}) while((s32[]{:T(128)}, f32[16,32]{0,1:T(8,128)S(1)}, s32[]{:T(128)}, s32[]{:T(128)}, s32[]{:T(128)}, /*index=5*/s32[]{:T(128)}) %tuple.337), condition=%wide.region_15.18_spmd.clone, body=%wide.region_14.17_spmd.clone.sunk | while | flops 1108 | bytes 5825 | solution.py:48
  611.7 24.0 %while.141 = (s32[]{:T(128)}, f32[16,32]{0,1:T(8,128)S(1)}, s32[]{:T(128)}, s32[]{:T(128)}, s32[]{:T(128)}, /*index=5*/s32[]{:T(128)}) while((s32[]{:T(128)}, f32[16,32]{0,1:T(8,128)S(1)}, s32[]{:T(128)}, s32[]{:T(128)}, s32[]{:T(128)}, /*index=5*/s32[]{:T(128)}) %tuple.340), condition=%wide.region_17.20_spmd.clone, body=%wide.region_16.19_spmd.clone.sunk | while | flops 1108 | bytes 5825 | solution.py:48
  637.1 24.0 %while.142 = (s32[]{:T(128)}, f32[16,32]{0,1:T(8,128)S(1)}, s32[]{:T(128)}, s32[]{:T(128)}, s32[]{:T(128)}, /*index=5*/s32[]{:T(128)}) while((s32[]{:T(128)}, f32[16,32]{0,1:T(8,128)S(1)}, s32[]{:T(128)}, s32[]{:T(128)}, s32[]{:T(128)}, /*index=5*/s32[]{:T(128)}) %tuple.343), condition=%wide.region_19.22_spmd.clone, body=%wide.region_18.21_spmd.clone.sunk | while | flops 1108 | bytes 5825 | solution.py:48
  661.7 24.0 %while.143 = (s32[]{:T(128)}, f32[16,32]{0,1:T(8,128)S(1)}, s32[]{:T(128)}, s32[]{:T(128)}, s32[]{:T(128)}, /*index=5*/s32[]{:T(128)}) while((s32[]{:T(128)}, f32[16,32]{0,1:T(8,128)S(1)}, s32[]{:T(128)}, s32[]{:T(128)}, s32[]{:T(128)}, /*index=5*/s32[]{:T(128)}) %tuple.346), condition=%wide.region_21.24_spmd.clone, body=%wide.region_20.23_spmd.clone.sunk | while | flops 1108 | bytes 5825 | solution.py:48
  688.1 7.6 convolution_bitcast_fusion
  696.0 65.7 %all-reduce.10.cloned.1.call-done = f32[512,128]{0,1:T(8,128)} async-done(((f32[512,128]{0,1:T(8,128)}), f32[512,128]{0,1:T(8,128)}) %all-reduce.10.cloned.1.call-update) | async-done | bytes 262160 | tf_op jit(solution)/shard_map/psum | solution.py:101
  761.7 1.6 fusion.132
  763.3 1.0 fusion.136
  764.6 139.2 %all-reduce.14.cloned.1.call-done = f32[128,128]{1,0:T(8,128)} async-done(((f32[128,128]{1,0:T(8,128)}), f32[128,128]{1,0:T(8,128)}) %all-reduce.14.cloned.1.call-update) | async-done | bytes 65552 | tf_op jit(solution)/shard_map/psum | solution.py:103
  903.9 1.2 fusion.131
  905.1 1.3 fusion.48
  906.4 1.5 convolution_negate_fusion
  907.9 98.7 %all-gather.5.cloned.1.call-done = f32[16384,128]{1,0:T(8,128)} async-done(((f32[512,128]{1,0:T(8,128)}), f32[16384,128]{1,0:T(8,128)}) %all-gather.5.cloned.1.call-update) | async-done | bytes 8388624 | tf_op jit(solution)/shard_map/all_gather | solution.py:106
  1006.7 5.0 fusion.49
  1011.7 6.7 subtract_subtract_fusion
  (608 shorter events, 195.8 us)
Async XLA Ops:
  7.2 1.0 copy-start
  7.2 145.8 %all-reduce.6.cloned.1.call-start = ((), (), s32[]{:S(2)}) async-start(), calls=%async_computation | async-start | bytes 131072 | tf_op jit(solution)/shard_map/psum | solution.py:86
  9.4 309.4 %all-reduce.8.cloned.1.call-start = ((), (), s32[]{:S(2)}) async-start(), calls=%async_computation.1 | async-start | bytes 131072 | tf_op jit(solution)/shard_map/psum | solution.py:89
  167.8 738.6 %copy-start.4 = (f32[128,128]{1,0:T(8,128)}, f32[128,128]{1,0:T(8,128)S(1)}, u32[]{:S(2)}) copy-start(f32[128,128]{1,0:T(8,128)S(1)} %get-tuple-element.926) | copy-start | bytes 196612
  179.1 305.8 %all-reduce.12.cloned.1.call-start = ((), (), s32[]{:S(2)}) async-start(), calls=%async_computation.4 | async-start | bytes 131072 | tf_op jit(solution)/shard_map/psum | solution.py:11
  345.1 343.0 %all-gather.3.cloned.1.call-start = ((), (), s32[]{:S(2)}) async-start(), calls=%async_computation.2 | async-start | bytes 8650752 | tf_op jit(solution)/shard_map/all_gather | solution.py:98
  345.7 416.0 %all-reduce.10.cloned.1.call-start = ((), (), s32[]{:S(2)}) async-start(), calls=%async_computation.3 | async-start | bytes 524288 | tf_op jit(solution)/shard_map/psum | solution.py:101
  637.1 126.1 %copy-start.2 = (f32[512,128]{0,1:T(8,128)S(1)}, f32[512,128]{0,1:T(8,128)}, u32[]{:S(2)}) copy-start(f32[512,128]{0,1:T(8,128)} %get-tuple-element.927) | copy-start | bytes 786436
  695.7 208.2 %all-reduce.14.cloned.1.call-start = ((), (), s32[]{:S(2)}) async-start(), calls=%async_computation.5 | async-start | bytes 131072 | tf_op jit(solution)/shard_map/psum | solution.py:103
  764.3 242.3 %all-gather.5.cloned.1.call-start = ((), (), s32[]{:S(2)}) async-start(), calls=%async_computation.6 | async-start | bytes 8650752 | tf_op jit(solution)/shard_map/all_gather | solution.py:106
  906.4 105.3 %copy-start.3 = (f32[512,128]{1,0:T(8,128)S(1)}, f32[512,128]{1,0:T(8,128)}, u32[]{:S(2)}) copy-start(f32[512,128]{1,0:T(8,128)} %fusion.48) | copy-start | bytes 786436
  1006.7 5.1 copy-start.1
Sparse Core Ops, SparseCore 0:
  12.0 140.8 all-reduce.5
  179.2 139.5 all-reduce.7
  345.3 139.6 all-reduce.11
  487.9 100.0 all-gather.2
  695.8 65.7 all-reduce.9
  765.6 138.2 all-reduce.13
  907.0 99.5 all-gather.4
where the time goes:
time: 1030 us
  waiting for transfers between devices  726 us (70%)
  other arithmetic  166 us (16%)
  local copies, waits for them, and re-layouts  79.2 us (8%)
  matrix products  37.4 us (4%)
  between operations  14.5 us (1%)
    psum x1, waiting for transfers between devices, body(): first_gram = lax.psum(gram_of(panel_block), 'row')  144 us
    psum x1, waiting for transfers between devices, body(): second_gram = lax.psum(gram_of(first_basis), 'row')  139 us
    psum x1, waiting for transfers between devices, body(): inner_sum = lax.psum(gram_both(vectors, applied), 'row')  139 us
    psum x1, waiting for transfers between devices, broadcast(): return lax.psum(jnp.where(mine, shard, jnp.zeros_like(shard)), axis)  139 us
    div x128, other arithmetic, eliminate(): pivot_row = pivot_row / pivot_row[pivot]  106 us
    all_gather x1, waiting for transfers between devices, body(): all_update = lax.all_gather(row_update, 'row', axis=0, tiled=True)  98.7 us
    dynamic_slice x128, local copies, waits for them, and re-layouts, eliminate(): pivot_row = pivot_row / pivot_row[pivot]  74.9 us
    psum x1, waiting for transfers between devices, body(): row_product = lax.psum(partial_product, 'col')  65.7 us
  transfers between devices with their start and end apart: 7, of which 6 were waited for; matrix products, arithmetic and copies ran while one was open for 20% of the time, Pallas kernels for 0%

commit v1 on v0

--- a/solution.py
+++ b/solution.py
@@ -86,7 +86,9 @@
     first_gram = lax.psum(gram_of(panel_block), "row")
     first_factor = jnp.linalg.cholesky(first_gram)
     first_basis = right_solve(first_factor, panel_block)
-    second_gram = lax.psum(gram_of(first_basis), "row")
+    part = gram_of(first_basis)
+    blocks = lax.all_gather(part, "row", axis=0, tiled=False)
+    second_gram = blocks.sum(axis=0)
     second_factor = jnp.linalg.cholesky(second_gram)
     basis = right_solve(second_factor, first_basis)
     top_basis = broadcast(basis[:panel_width], "row", 0)

time: 1030 us -> 962 us (0.934)
  waiting for transfers between devices: 726 us -> 662 us
    psum x1 -> x0, waiting for transfers between devices: 139 us -> none  [body(): second_gram = lax.psum(gram_of(first_basis), 'row')]
    all_gather x0 -> x1, waiting for transfers between devices: none -> 75.7 us  [body(): blocks = lax.all_gather(part, 'row', axis=0, tiled=False)]
  transfers between devices with their start and end apart: 7 -> 7, of which waited for: 6 -> 6; matrix products, arithmetic and copies ran while one was open for 20% -> 21% of each run, Pallas kernels for 0% -> 0%
where the time goes in v1:
time: 962 us; the launch traced here: 961 us
  waiting for transfers between devices  662 us (69%)
  other arithmetic  167 us (17%)
  local copies, waits for them, and re-layouts  78.3 us (8%)
  matrix products  37.4 us (4%)
  between operations  14.5 us (2%)
    psum x1, waiting for transfers between devices, body(): first_gram = lax.psum(gram_of(panel_block), 'row')  144 us
    psum x1, waiting for transfers between devices, body(): inner_sum = lax.psum(gram_both(vectors, applied), 'row')  139 us
    psum x1, waiting for transfers between devices, broadcast(): return lax.psum(jnp.where(mine, shard, jnp.zeros_like(shard)), axis)  138 us
    div x128, other arithmetic, eliminate(): pivot_row = pivot_row / pivot_row[pivot]  106 us
    all_gather x1, waiting for transfers between devices, body(): all_update = lax.all_gather(row_update, 'row', axis=0, tiled=True)  98.7 us
    all_gather x1, waiting for transfers between devices, body(): blocks = lax.all_gather(part, 'row', axis=0, tiled=False)  75.7 us
    dynamic_slice x128, local copies, waits for them, and re-layouts, eliminate(): pivot_row = pivot_row / pivot_row[pivot]  74.9 us
    psum x1, waiting for transfers between devices, body(): row_product = lax.psum(partial_product, 'col')  65.7 us
  transfers between devices with their start and end apart: 7, of which 6 were waited for; matrix products, arithmetic and copies ran while one was open for 21% of the time, Pallas kernels for 0%

profile of v1, /device:TPU:1, one launch (start us, length us, event | category | flops | bytes accessed | tf_op | source)
XLA Modules:
  0.0 960.8 jit_solution(15597322216782677483)
XLA Ops:
  7.2 0.9 copy-done
  8.1 1.2 fusion.134
  9.4 143.5 %all-reduce.5.cloned.1.call-done = f32[128,128]{0,1:T(8,128)} async-done(((f32[128,128]{0,1:T(8,128)}), f32[128,128]{0,1:T(8,128)}) %all-reduce.5.cloned.1.call-update) | async-done | bytes 65552 | tf_op jit(solution)/shard_map/psum | solution.py:86
  152.9 0.9 copy.44
  153.9 0.9 fusion.57
  154.7 11.7 %cholesky.44 = f32[128,128]{1,0:T(8,128)S(1)} custom-call(f32[128,128]{1,0:T(8,128)S(1)} %fusion.57), custom_call_target="Cholesky" | custom-call | tf_op jit(solution)/shard_map/jit(cholesky)/cholesky | solution.py:87
  167.8 9.8 %custom-call.6 = f32[1,128,128]{1,2,0:T(8,128)S(1)} custom-call(f32[1,128,128]{2,1,0:T(8,128)S(1)} %get-tuple-element.941), custom_call_target="InvertDiagBlocksLowerTriangular" | custom-call | tf_op jit(solution)/shard_map/triangular_solve/custom-call.0 | solution.py:75
  178.0 1.0 fusion.135
  179.3 75.7 %all-gather.9.cloned.1.call-done = f32[4096,128]{1,0:T(8,128)} async-done(((f32[128,128]{1,0:T(8,128)}), f32[4096,128]{1,0:T(8,128)}) %all-gather.9.cloned.1.call-update) | async-done | bytes 2097168 | tf_op jit(solution)/shard_map/all_gather | solution.py:90
  255.0 1.7 reduce_sum.9
  256.8 11.7 %cholesky.55 = f32[128,128]{1,0:T(8,128)S(1)} custom-call(f32[128,128]{1,0:T(8,128)S(1)} %fusion.55), custom_call_target="Cholesky" | custom-call | tf_op jit(solution)/shard_map/jit(cholesky)/cholesky | solution.py:92
  269.8 9.8 %custom-call.7 = f32[1,128,128]{1,2,0:T(8,128)S(1)} custom-call(f32[1,128,128]{2,1,0:T(8,128)S(1)} %select_bitcast_fusion), custom_call_target="InvertDiagBlocksLowerTriangular" | custom-call | tf_op jit(solution)/shard_map/triangular_solve/custom-call.0 | solution.py:75
  279.6 1.1 convert_add_fusion
  282.2 138.2 %all-reduce.9.cloned.1.call-done = f32[128,128]{1,0:T(8,128)} async-done(((f32[128,128]{1,0:T(8,128)}), f32[128,128]{1,0:T(8,128)}) %all-reduce.9.cloned.1.call-update) | async-done | bytes 65552 | tf_op jit(solution)/shard_map/psum | solution.py:11
  420.5 0.9 fusion.65
  421.5 24.0 %while.136 = (s32[]{:T(128)}, f32[16,32]{0,1:T(8,128)S(1)}, s32[]{:T(128)}, s32[]{:T(128)}, s32[]{:T(128)}, /*index=5*/s32[]{:T(128)}) while((s32[]{:T(128)}, f32[16,32]{0,1:T(8,128)S(1)}, s32[]{:T(128)}, s32[]{:T(128)}, s32[]{:T(128)}, /*index=5*/s32[]{:T(128)}) %tuple.333), condition=%wide.region_7.10_spmd.clone, body=%wide.region_6.9_spmd.clone.sunk | while | flops 1108 | bytes 5825 | solution.py:48
  437.1 0.8 fusion.206
  438.6 0.8 fusion.206
  441.6 0.8 fusion.206
  444.6 0.8 fusion.206
  446.3 24.0 %while.137 = (s32[]{:T(128)}, f32[16,32]{0,1:T(8,128)S(1)}, s32[]{:T(128)}, s32[]{:T(128)}, s32[]{:T(128)}, /*index=5*/s32[]{:T(128)}) while((s32[]{:T(128)}, f32[16,32]{0,1:T(8,128)S(1)}, s32[]{:T(128)}, s32[]{:T(128)}, s32[]{:T(128)}, /*index=5*/s32[]{:T(128)}) %tuple.336), condition=%wide.region_9.12_spmd.clone, body=%wide.region_8.11_spmd.clone.sunk | while | flops 1108 | bytes 5825 | solution.py:48
  451.4 0.8 fusion.208
  455.9 0.8 fusion.208
  457.4 0.8 fusion.208
  471.8 24.0 %while.138 = (s32[]{:T(128)}, f32[16,32]{0,1:T(8,128)S(1)}, s32[]{:T(128)}, s32[]{:T(128)}, s32[]{:T(128)}, /*index=5*/s32[]{:T(128)}) while((s32[]{:T(128)}, f32[16,32]{0,1:T(8,128)S(1)}, s32[]{:T(128)}, s32[]{:T(128)}, s32[]{:T(128)}, /*index=5*/s32[]{:T(128)}) %tuple.339), condition=%wide.region_11.14_spmd.clone, body=%wide.region_10.13_spmd.clone.sunk | while | flops 1108 | bytes 5825 | solution.py:48
  475.4 0.8 fusion.210
  476.9 0.8 fusion.210
  485.9 0.8 fusion.210
  488.9 0.8 fusion.210
  491.9 0.8 fusion.210
  496.6 24.0 %while.139 = (s32[]{:T(128)}, f32[16,32]{0,1:T(8,128)S(1)}, s32[]{:T(128)}, s32[]{:T(128)}, s32[]{:T(128)}, /*index=5*/s32[]{:T(128)}) while((s32[]{:T(128)}, f32[16,32]{0,1:T(8,128)S(1)}, s32[]{:T(128)}, s32[]{:T(128)}, s32[]{:T(128)}, /*index=5*/s32[]{:T(128)}) %tuple.342), condition=%wide.region_13.16_spmd.clone, body=%wide.region_12.15_spmd.clone.sunk | while | flops 1108 | bytes 5825 | solution.py:48
  497.2 0.8 fusion.212
  503.2 0.8 fusion.212
  522.6 24.0 %while.140 = (s32[]{:T(128)}, f32[16,32]{0,1:T(8,128)S(1)}, s32[]{:T(128)}, s32[]{:T(128)}, s32[]{:T(128)}, /*index=5*/s32[]{:T(128)}) while((s32[]{:T(128)}, f32[16,32]{0,1:T(8,128)S(1)}, s32[]{:T(128)}, s32[]{:T(128)}, s32[]{:T(128)}, /*index=5*/s32[]{:T(128)}) %tuple.345), condition=%wide.region_15.18_spmd.clone, body=%wide.region_14.17_spmd.clone.sunk | while | flops 1108 | bytes 5825 | solution.py:48
  547.2 24.0 %while.141 = (s32[]{:T(128)}, f32[16,32]{0,1:T(8,128)S(1)}, s32[]{:T(128)}, s32[]{:T(128)}, s32[]{:T(128)}, /*index=5*/s32[]{:T(128)}) while((s32[]{:T(128)}, f32[16,32]{0,1:T(8,128)S(1)}, s32[]{:T(128)}, s32[]{:T(128)}, s32[]{:T(128)}, /*index=5*/s32[]{:T(128)}) %tuple.348), condition=%wide.region_17.20_spmd.clone, body=%wide.region_16.19_spmd.clone.sunk | while | flops 1108 | bytes 5825 | solution.py:48
  572.7 24.0 %while.142 = (s32[]{:T(128)}, f32[16,32]{0,1:T(8,128)S(1)}, s32[]{:T(128)}, s32[]{:T(128)}, s32[]{:T(128)}, /*index=5*/s32[]{:T(128)}) while((s32[]{:T(128)}, f32[16,32]{0,1:T(8,128)S(1)}, s32[]{:T(128)}, s32[]{:T(128)}, s32[]{:T(128)}, /*index=5*/s32[]{:T(128)}) %tuple.351), condition=%wide.region_19.22_spmd.clone, body=%wide.region_18.21_spmd.clone.sunk | while | flops 1108 | bytes 5825 | solution.py:48
  597.3 24.0 %while.143 = (s32[]{:T(128)}, f32[16,32]{0,1:T(8,128)S(1)}, s32[]{:T(128)}, s32[]{:T(128)}, s32[]{:T(128)}, /*index=5*/s32[]{:T(128)}) while((s32[]{:T(128)}, f32[16,32]{0,1:T(8,128)S(1)}, s32[]{:T(128)}, s32[]{:T(128)}, s32[]{:T(128)}, /*index=5*/s32[]{:T(128)}) %tuple.354), condition=%wide.region_21.24_spmd.clone, body=%wide.region_20.23_spmd.clone.sunk | while | flops 1108 | bytes 5825 | solution.py:48
  623.7 7.6 convolution_bitcast_fusion
  631.5 65.7 %all-reduce.7.cloned.1.call-done = f32[512,128]{0,1:T(8,128)} async-done(((f32[512,128]{0,1:T(8,128)}), f32[512,128]{0,1:T(8,128)}) %all-reduce.7.cloned.1.call-update) | async-done | bytes 262160 | tf_op jit(solution)/shard_map/psum | solution.py:103
  697.2 1.6 fusion.132
  698.8 1.0 fusion.136
  700.2 139.2 %all-reduce.11.cloned.1.call-done = f32[128,128]{1,0:T(8,128)} async-done(((f32[128,128]{1,0:T(8,128)}), f32[128,128]{1,0:T(8,128)}) %all-reduce.11.cloned.1.call-update) | async-done | bytes 65552 | tf_op jit(solution)/shard_map/psum | solution.py:105
  839.4 1.2 fusion.131
  840.6 1.3 fusion.48
  842.0 1.5 convolution_negate_fusion
  843.5 98.7 %all-gather.7.cloned.1.call-done = f32[16384,128]{1,0:T(8,128)} async-done(((f32[512,128]{1,0:T(8,128)}), f32[16384,128]{1,0:T(8,128)}) %all-gather.7.cloned.1.call-update) | async-done | bytes 8388624 | tf_op jit(solution)/shard_map/all_gather | solution.py:108
  942.2 5.0 fusion.49
  947.3 6.7 subtract_subtract_fusion
  (609 shorter events, 195.1 us)
Async XLA Ops:
  7.2 1.0 copy-start
  7.2 145.8 %all-reduce.5.cloned.1.call-start = ((), (), s32[]{:S(2)}) async-start(), calls=%async_computation | async-start | bytes 131072 | tf_op jit(solution)/shard_map/psum | solution.py:86
  9.4 245.6 %all-gather.9.cloned.1.call-start = ((), (), s32[]{:S(2)}) async-start(), calls=%async_computation.6 | async-start | bytes 2162688 | tf_op jit(solution)/shard_map/all_gather | solution.py:90
  167.8 674.2 %copy-start.4 = (f32[128,128]{1,0:T(8,128)}, f32[128,128]{1,0:T(8,128)S(1)}, u32[]{:S(2)}) copy-start(f32[128,128]{1,0:T(8,128)S(1)} %get-tuple-element.942) | copy-start | bytes 196612
  179.1 241.4 %all-reduce.9.cloned.1.call-start = ((), (), s32[]{:S(2)}) async-start(), calls=%async_computation.3 | async-start | bytes 131072 | tf_op jit(solution)/shard_map/psum | solution.py:11
  281.4 342.3 %all-gather.5.cloned.1.call-start = ((), (), s32[]{:S(2)}) async-start(), calls=%async_computation.1 | async-start | bytes 8650752 | tf_op jit(solution)/shard_map/all_gather | solution.py:100
  282.0 415.2 %all-reduce.7.cloned.1.call-start = ((), (), s32[]{:S(2)}) async-start(), calls=%async_computation.2 | async-start | bytes 524288 | tf_op jit(solution)/shard_map/psum | solution.py:103
  572.7 126.1 %copy-start.2 = (f32[512,128]{0,1:T(8,128)S(1)}, f32[512,128]{0,1:T(8,128)}, u32[]{:S(2)}) copy-start(f32[512,128]{0,1:T(8,128)} %get-tuple-element.943) | copy-start | bytes 786436
  631.3 208.2 %all-reduce.11.cloned.1.call-start = ((), (), s32[]{:S(2)}) async-start(), calls=%async_computation.4 | async-start | bytes 131072 | tf_op jit(solution)/shard_map/psum | solution.py:105
  699.9 242.3 %all-gather.7.cloned.1.call-start = ((), (), s32[]{:S(2)}) async-start(), calls=%async_computation.5 | async-start | bytes 8650752 | tf_op jit(solution)/shard_map/all_gather | solution.py:108
  841.9 105.3 %copy-start.3 = (f32[512,128]{1,0:T(8,128)S(1)}, f32[512,128]{1,0:T(8,128)}, u32[]{:S(2)}) copy-start(f32[512,128]{1,0:T(8,128)} %fusion.48) | copy-start | bytes 786436
  942.2 5.1 copy-start.1
Sparse Core Ops, SparseCore 0:
  12.0 140.8 all-reduce.4
  179.2 75.7 all-gather.8
  281.5 138.8 all-reduce.8
  423.5 100.0 all-gather.4
  631.4 65.7 all-reduce.6
  701.1 138.2 all-reduce.10
  842.6 99.5 all-gather.6
